TPU v7x, 32 devices: a whole 2x2x4 slice. The times are simulated.
32 devices in a mesh: rep: 4 (over x, core), own: 8 (over z, y).
Axes of the slice: x: 2, y: 2, z: 4, core: 2. Of those that a mesh axis runs over, the one named last changes fastest.
Arguments:
- weights: float32 [4, 256, 8, 2048], P('rep', 'own'), may hold values from -6 to 6
- anchor: float32 [832, 8, 2048], P('own'), may hold values from -6 to 6
- momentum: float32 [832, 8, 2048], P('own'), may hold values from -3 to 3
- owner: int32 [256], replicated, may hold values from 0 to 7, as said below
- emb_weights: float32 [4, 1024, 2048], P('rep', 'own'), may hold values from -6 to 6
- emb_anchor: float32 [1024, 2048], P('own'), may hold values from -6 to 6
- emb_momentum: float32 [1024, 2048], P('own'), may hold values from -3 to 3
- sketch: float32 [64, 2048], replicated, may hold values from -0.125 to 0.125
- inv_root: float32 [64, 64], replicated
Outputs:
- new_weights: float32 [256, 8, 2048], P('own')
- new_momentum: float32 [832, 8, 2048], P('own')
- new_embedding: float32 [1024, 2048], P('own')
- new_emb_momentum: float32 [1024, 2048], P('own')
Inputs may be any that keep to these rules, and one draw needn't show every extreme that they name: Each owner holds at least 8 and at most 104 tiles, and some owner holds exactly 104. Of the 32 tiles of one aligned block, at most 13 have the same owner, and some block reaches 13.
All inputs are finite; a program needn't handle non-finite values.
Results may differ from a plain program's by a relative error of at most 0.0001.
Values sent between devices are 32-bit elements; how exact they have to be, the bound alone decides.
A program may use at most 128 MiB of HBM per device.

v0:
```python
import jax
import jax.numpy as jnp
from jax import lax
from jax.sharding import PartitionSpec as P

OUTER_RATE = 0.7
OUTER_MOMENTUM = 0.9


def owner_tables(owner, tiles_dev, per_pair, capacity, own_index, own_count):
    tile_count = owner.shape[0]
    tile_ids = jnp.arange(tile_count, dtype=jnp.int32)
    block_of = tile_ids // tiles_dev
    same_owner = owner[:, None] == owner[None, :]
    earlier = tile_ids[None, :] < tile_ids[:, None]
    slot_rank = jnp.sum(same_owner & earlier, axis=1, dtype=jnp.int32)
    pair_rank = jnp.sum(
        same_owner & earlier & (block_of[:, None] == block_of[None, :]), axis=1, dtype=jnp.int32
    )
    local_owner = lax.dynamic_slice_in_dim(owner, own_index * tiles_dev, tiles_dev)
    local_pair = lax.dynamic_slice_in_dim(pair_rank, own_index * tiles_dev, tiles_dev)
    dest_ids = jnp.arange(own_count, dtype=jnp.int32)[:, None, None]
    pair_ids = jnp.arange(per_pair, dtype=jnp.int32)[None, :, None]
    outgoing_match = (local_owner[None, None, :] == dest_ids) & (
        local_pair[None, None, :] == pair_ids
    )
    local_ids = jnp.arange(tiles_dev, dtype=jnp.int32)[None, None, :]
    local_pick = jnp.sum(jnp.where(outgoing_match, local_ids, 0), axis=2).reshape(-1)
    shard_read = local_owner * per_pair + local_pair
    held_here = owner == own_index
    slot_ids = jnp.arange(capacity, dtype=jnp.int32)[:, None]
    holder_match = held_here[None, :] & (slot_rank[None, :] == slot_ids)
    owner_read = jnp.sum(
        jnp.where(holder_match, (block_of * per_pair + pair_rank)[None, :], 0), axis=1
    )
    is_filled = jnp.any(holder_match, axis=1)
    return_match = (
        held_here[None, None, :]
        & (block_of[None, None, :] == dest_ids)
        & (pair_rank[None, None, :] == pair_ids)
    )
    owner_pick = jnp.sum(jnp.where(return_match, slot_rank[None, None, :], 0), axis=2).reshape(-1)
    return (local_pick, shard_read, owner_read, is_filled, owner_pick)


def local(
    weights, anchor, momentum, owner, emb_weights, emb_anchor, emb_momentum, sketch, inv_root
):
    own_count = lax.axis_size("own")
    rep_count = lax.axis_size("rep")
    own_index = lax.axis_index("own")
    tiles_dev = weights.shape[1]
    tile_rows = weights.shape[2]
    width = weights.shape[3]
    capacity = anchor.shape[0]
    half_tiles = min(tiles_dev // 2, own_count)
    hot_count = max(own_count // 4, 1)
    per_pair = (tiles_dev - half_tiles) // hot_count + 1
    local_pick, shard_read, owner_read, is_filled, owner_pick = owner_tables(
        owner, tiles_dev, per_pair, capacity, own_index, own_count
    )
    rep_index = lax.axis_index("rep")
    part = width // rep_count
    mean_part = lax.psum_scatter(weights[0], "rep", scatter_dimension=2, tiled=True) * (
        1.0 / rep_count
    )
    anchor_part = lax.dynamic_slice_in_dim(anchor, rep_index * part, part, axis=2)
    momentum_part = lax.dynamic_slice_in_dim(momentum, rep_index * part, part, axis=2)
    held_part = anchor_part - OUTER_RATE * (
        (1.0 + OUTER_MOMENTUM) * anchor_part + OUTER_MOMENTUM * OUTER_MOMENTUM * momentum_part
    )

    def exchange(tiles, pick):
        sent = jnp.take(tiles, pick, axis=0).reshape(own_count, per_pair, tile_rows, part)
        return lax.all_to_all(sent, "own", split_axis=0, concat_axis=0, tiled=True).reshape(
            own_count * per_pair, tile_rows, part
        )

    landed = jnp.take(exchange(held_part, owner_pick), shard_read, axis=0)
    new_part = landed + OUTER_RATE * (1.0 + OUTER_MOMENTUM) * mean_part
    placed_part = jnp.take(exchange(mean_part, local_pick), owner_read, axis=0)
    new_weights = lax.all_gather(new_part, "rep", axis=2, tiled=True)
    weight_mean = lax.all_gather(placed_part, "rep", axis=2, tiled=True)
    moved = OUTER_MOMENTUM * momentum + (anchor - weight_mean)
    new_momentum = jnp.where(is_filled[:, None, None], moved, 0.0)
    highest = lax.Precision.HIGHEST
    emb_diff = emb_anchor - emb_weights[0]
    local_sketch = lax.dot_general(
        sketch,
        emb_diff,
        (((1,), (1,)), ((), ())),
        precision=highest,
        preferred_element_type=jnp.float32,
    )
    sketch_mean = lax.psum(local_sketch, "rep") * (1.0 / rep_count)
    basis_rows = jnp.dot(
        inv_root, sketch_mean, precision=highest, preferred_element_type=jnp.float32
    )
    local_factor = jnp.dot(
        basis_rows, emb_diff, precision=highest, preferred_element_type=jnp.float32
    )
    factor = lax.psum(local_factor, ("rep", "own")) * (1.0 / rep_count)
    approx = lax.dot_general(
        basis_rows,
        factor,
        (((0,), (0,)), ((), ())),
        precision=highest,
        preferred_element_type=jnp.float32,
    )
    new_emb_momentum = OUTER_MOMENTUM * emb_momentum + approx
    new_embedding = emb_anchor - OUTER_RATE * (approx + OUTER_MOMENTUM * new_emb_momentum)
    return (new_weights, new_momentum, new_embedding, new_emb_momentum)


def solution(mesh):
    placed = (
        P("rep", "own", None, None),
        P("own", None, None),
        P("own", None, None),
        P(),
        P("rep", "own", None),
        P("own", None),
        P("own", None),
        P(),
        P(),
    )
    return jax.shard_map(
        local,
        mesh=mesh,
        in_specs=placed,
        out_specs=(P("own", None, None), P("own", None, None), P("own", None), P("own", None)),
        check_vma=False,
    )
```

profile of v0, /device:TPU:0, one launch (start us, length us, event | category | flops | bytes accessed | tf_op | source)
XLA Modules:
  0.0 231.5 jit_solution(14581863288011839253)
XLA Ops:
  8.0 0.0 copy-start
  8.0 0.0 copy-start.6
  8.0 0.0 reduce-scatter.2.cloned.1.call-start
  8.1 0.7 reduce-scatter.2.cloned.1.call-update
  8.8 0.0 copy-done.6
  8.8 0.3 convert_reduce_fusion.1
  9.1 0.3 select_reduce_fusion.1
  9.4 0.1 copy.13
  9.5 0.1 reshape.229
  9.6 3.6 %multiply_subtract_fusion = f32[104,8,512]{2,1,0:T(8,128)} fusion(f32[104,8,2048]{2,1,0:T(8,128)} %param.13, s32[]{:T(128)S(6)} %select_n.88, f32[104,8,2048]{2,1,0:T(8,128)} %param.12), kind=kLoop, calls=%fused_computation.5 | loop fusion | flops 2129920 | bytes 5111812 | tf_op jit(solution)/shard_map/sub | solution.py:69
  13.2 2.1 gather_fusion.2
  15.3 1.4 broadcast_select_fusion.1
  16.7 0.0 copy-start.1
  16.7 0.0 copy-start.2
  16.7 7.5 %all-to-all-start = ((f32[8,13,8,512]{3,2,1,0:T(8,128)}), f32[8,13,8,512]{3,2,1,0:T(8,128)}, u32[]{:S(2)}, u32[]{:S(2)}) async-start(f32[8,13,8,512]{3,2,1,0:T(8,128)} %bitcast), calls=%async_computation | async-start | bytes 3407872 | tf_op jit(solution)/shard_map/all_to_all | solution.py:75
  24.2 0.0 copy-start.5
  24.2 0.0 all-reduce.2.cloned.1.call-start
  24.3 0.0 copy-done
  24.3 0.0 copy-done.1
  24.3 0.0 copy-done.2
  24.3 1.2 convolution_bitcast_fusion
  25.5 11.7 %psum.14 = f32[64,128]{1,0:T(8,128)S(1)} all-reduce(f32[64,128]{1,0:T(8,128)S(1)} %convolution_bitcast_fusion), channel_id=1, replica_groups=mesh['rep'=4,'own'=8] {'rep'}, use_global_device_ids=true, to_apply=%region_7.9 | all-reduce | flops 8192 | bytes 65536 | tf_op jit(solution)/shard_map/psum | solution.py:95
  37.2 0.0 copy-done.5
  37.2 0.2 fusion.7
  37.3 1.5 fusion.2
  38.9 0.0 all-reduce.2.cloned.1.call-update
  38.9 0.1 compare_and_fusion.3
  39.0 0.3 select_reduce_fusion.2
  39.3 0.1 copy.15
  39.4 0.1 reshape.232
  39.5 0.1 copy.14
  39.6 25.8 %all-to-all-done = f32[8,13,8,512]{3,2,1,0:T(8,128)} async-done(((f32[8,13,8,512]{3,2,1,0:T(8,128)}), f32[8,13,8,512]{3,2,1,0:T(8,128)}, u32[]{:S(2)}, u32[]{:S(2)}) %all-to-all-start) | async-done | bytes 1703968 | tf_op jit(solution)/shard_map/all_to_all | solution.py:75
  65.5 2.0 gather_fusion
  67.5 0.0 reduce-scatter.2.cloned.1.call-done
  67.5 2.0 broadcast_multiply_fusion
  69.5 1.9 gather_fusion.1
  71.5 2.8 %broadcast_select_fusion.2 = f32[8,13,8,512]{3,2,1,0:T(8,128)} fusion(f32[8,13,8,512]{3,2,1,0:T(8,128)} %bitcast.17, pred[8,13]{1,0:T(8,128)(4,1)S(1)} %copy.14), kind=kLoop, calls=%fused_computation.12 | loop fusion | flops 425984 | bytes 3407976 | tf_op jit(solution)/shard_map/jit(_take)/select_n | solution.py:74
  74.3 3.7 %all-to-all-start.1 = ((f32[8,13,8,512]{3,2,1,0:T(8,128)}), f32[8,13,8,512]{3,2,1,0:T(8,128)S(1)}, u32[]{:S(2)}, u32[]{:S(2)}) async-start(f32[8,13,8,512]{3,2,1,0:T(8,128)} %broadcast_select_fusion.2), calls=%async_computation.2 | async-start | bytes 3407872 | tf_op jit(solution)/shard_map/all_to_all | solution.py:75
  78.0 0.0 all-gather.3.cloned.1.call-start
  78.0 0.7 all-gather.3.cloned.1.call-update
  78.7 0.0 all-gather.5.cloned.1.call-start
  78.8 0.1 select_reduce_fusion
  78.9 39.9 %all-to-all-done.1 = f32[8,13,8,512]{3,2,1,0:T(8,128)S(1)} async-done(((f32[8,13,8,512]{3,2,1,0:T(8,128)}), f32[8,13,8,512]{3,2,1,0:T(8,128)S(1)}, u32[]{:S(2)}, u32[]{:S(2)}) %all-to-all-start.1) | async-done | bytes 1703968 | tf_op jit(solution)/shard_map/all_to_all | solution.py:75
  118.9 1.9 gather_fusion.3
  120.8 2.8 %broadcast_select_fusion = f32[104,8,512]{2,1,0:T(8,128)} fusion(f32[104,8,512]{2,1,0:T(8,128)} %gather_fusion.3, pred[104]{0:T(512)(128)(4,1)S(1)} %compare_and_fusion.1), kind=kLoop, calls=%fused_computation.10 | loop fusion | flops 425984 | bytes 3407976 | tf_op jit(solution)/shard_map/jit(_take)/select_n | solution.py:81
  123.6 0.0 copy-start.4
  123.6 0.0 all-gather.5.cloned.1.call-update
  123.7 0.1 fusion.6
  123.8 84.6 %all-reduce.2.cloned.1.call-done = f32[64,2048]{1,0:T(8,128)} async-done(((f32[64,2048]{1,0:T(8,128)}), f32[64,2048]{1,0:T(8,128)}) %all-reduce.2.cloned.1.call-update) | async-done | bytes 524304 | tf_op jit(solution)/shard_map/psum | solution.py:102
  208.4 0.0 copy-done.4
  208.4 3.6 %multiply_subtract_fusion.1 = (f32[128,2048]{1,0:T(8,128)}, f32[128,2048]{1,0:T(8,128)}) fusion(f32[128,2048]{1,0:T(8,128)S(1)} %copy-done.1, f32[128,2048]{1,0:T(8,128)S(1)} %copy-done.4, f32[128,64]{0,1:T(8,128)S(1)} %fusion.7, f32[64,2048]{1,0:T(8,128)} %all-reduce.2.cloned.1.call-done), kind=kOutput, calls=%fused_computation.8 | convolution fusion | flops 203030528 | bytes 4751360 | tf_op jit(solution)/shard_map/dot_general | solution.py:103
  212.0 0.0 all-gather.3.cloned.1.call-done
  212.0 0.0 all-gather.5.cloned.1.call-done
  212.0 0.0 copy-start.3
  212.0 11.0 %add_select_fusion = f32[104,8,2048]{2,1,0:T(8,128)} fusion(f32[104,8,2048]{2,1,0:T(8,128)} %param.12, f32[104,8,2048]{2,1,0:T(8,128)} %all-gather.5.cloned.1.call-done, f32[104,8,2048]{2,1,0:T(8,128)} %param.13, pred[104]{0:T(512)(128)(4,1)S(1)} %fusion.6), kind=kLoop, calls=%fused_computation.4 | loop fusion | flops 6815744 | bytes 27263080 | tf_op jit(solution)/shard_map/jit(_where)/select_n | solution.py:85
  223.0 0.0 copy-done.3
  223.0 1.3 copy.18
  (17 shorter events, 0.1 us)
Async XLA Ops:
  8.0 16.3 %copy-start = (f32[64,2048]{1,0:T(8,128)S(1)}, f32[64,2048]{1,0:T(8,128)}, u32[]{:S(2)}) copy-start(f32[64,2048]{1,0:T(8,128)} %param.18) | copy-start | bytes 1572868
  8.0 0.8 copy-start.6
  8.0 59.5 %reduce-scatter.2.cloned.1.call-start = ((), (), s32[]{:S(2)}) async-start(), calls=%async_computation.3 | async-start | bytes 2621440 | tf_op jit(solution)/shard_map/reduce_scatter | solution.py:64
  16.7 7.6 %copy-start.1 = (f32[128,2048]{1,0:T(8,128)S(1)}, f32[128,2048]{1,0:T(8,128)}, u32[]{:S(2)}) copy-start(f32[128,2048]{1,0:T(8,128)} %param.16) | copy-start | bytes 3145732
  16.7 7.6 %copy-start.2 = (f32[1,128,2048]{2,1,0:T(8,128)S(1)}, f32[1,128,2048]{2,1,0:T(8,128)}, u32[]{:S(2)}) copy-start(f32[1,128,2048]{2,1,0:T(8,128)} %param.15) | copy-start | bytes 3145732
  16.7 48.8 %all-to-all-start = ((f32[8,13,8,512]{3,2,1,0:T(8,128)}), f32[8,13,8,512]{3,2,1,0:T(8,128)}, u32[]{:S(2)}, u32[]{:S(2)}) async-start(f32[8,13,8,512]{3,2,1,0:T(8,128)} %bitcast), calls=%async_computation | async-start | bytes 3407872 | tf_op jit(solution)/shard_map/all_to_all | solution.py:75
  24.2 12.9 %copy-start.5 = (f32[64,64]{1,0:T(8,128)S(1)}, f32[64,64]{1,0:T(8,128)}, u32[]{:S(2)}) copy-start(f32[64,64]{1,0:T(8,128)} %param.19) | copy-start | bytes 49156
  24.2 184.2 %all-reduce.2.cloned.1.call-start = ((), (), s32[]{:S(2)}) async-start(), calls=%async_computation.6 | async-start | bytes 1048576 | tf_op jit(solution)/shard_map/psum | solution.py:102
  74.3 44.6 %all-to-all-start.1 = ((f32[8,13,8,512]{3,2,1,0:T(8,128)}), f32[8,13,8,512]{3,2,1,0:T(8,128)S(1)}, u32[]{:S(2)}, u32[]{:S(2)}) async-start(f32[8,13,8,512]{3,2,1,0:T(8,128)} %broadcast_select_fusion.2), calls=%async_computation.2 | async-start | bytes 3407872 | tf_op jit(solution)/shard_map/all_to_all | solution.py:75
  78.0 134.0 %all-gather.3.cloned.1.call-start = ((), (), s32[]{:S(2)}) async-start(), calls=%async_computation.4 | async-start | bytes 2621440 | tf_op jit(solution)/shard_map/all_gather | solution.py:82
  78.7 133.3 %all-gather.5.cloned.1.call-start = ((), (), s32[]{:S(2)}) async-start(), calls=%async_computation.5 | async-start | bytes 8519680 | tf_op jit(solution)/shard_map/all_gather | solution.py:83
  123.6 84.8 %copy-start.4 = (f32[128,2048]{1,0:T(8,128)S(1)}, f32[128,2048]{1,0:T(8,128)}, u32[]{:S(2)}) copy-start(f32[128,2048]{1,0:T(8,128)} %param.17) | copy-start | bytes 3145732
  212.0 11.0 %copy-start.3 = (f32[32,8,2048]{2,1,0:T(8,128)S(1)}, f32[32,8,2048]{2,1,0:T(8,128)}, u32[]{:S(2)}) copy-start(f32[32,8,2048]{2,1,0:T(8,128)} %all-gather.3.cloned.1.call-done) | copy-start | bytes 6291460
Sparse Core Ops, SparseCore 0:
  11.4 34.3 reduce-scatter.1
  81.0 23.9 all-gather.2
  123.8 48.6 all-gather.4
Sparse Core Ops, SparseCore 1:
  39.0 169.4 all-reduce.1
where the time goes:
time: 232 us; the launch traced here: 231 us
  waiting for transfers between devices  152 us (66%)
  other arithmetic  25 us (11%)
  between operations  15.4 us (7%)
  blocking collectives  11.7 us (5%)
  starting transfers between devices  11.4 us (5%)
  local copies, waits for them, and re-layouts  9.77 us (4%)
  matrix products  6.43 us (3%)
    psum x1, waiting for transfers between devices, local(): factor = lax.psum(local_factor, ('rep', 'own')) * (1.0 / rep_count)  84.6 us
    all_to_all x2, waiting for transfers between devices, exchange(): lax.all_to_all(sent, 'own', split_axis=0, concat_axis=0, tiled=True)  65.8 us
    psum x1, blocking collectives, local(): sketch_mean = lax.psum(local_sketch, 'rep') * (1.0 / rep_count)  11.7 us
    all_to_all x2, starting transfers between devices, exchange(): lax.all_to_all(sent, 'own', split_axis=0, concat_axis=0, tiled=True)  11.2 us
    select_n x1, other arithmetic, local(): new_momentum = jnp.where(is_filled[:, None, None], moved, 0.0)  11 us
  transfers between devices with their start and end apart: 6, of which 3 were waited for; matrix products, arithmetic and copies ran while one was open for 12% of the time, Pallas kernels for 0%

commit v1 on v0

--- a/solution.py
+++ b/solution.py
@@ -99,7 +99,7 @@
     local_factor = jnp.dot(
         basis_rows, emb_diff, precision=highest, preferred_element_type=jnp.float32
     )
-    factor = lax.psum(local_factor, ("rep", "own")) * (1.0 / rep_count)
+    factor = jax.lax.psum(jax.lax.psum(local_factor, "own"), "rep") * (1.0 / rep_count)
     approx = lax.dot_general(
         basis_rows,
         factor,

time: 232 us -> 249 us (1.073)
  waiting for transfers between devices: 152 us -> 166 us
    all_gather x1, waiting for transfers between devices: 0.01 us -> 48 us  [local(): weight_mean = lax.all_gather(placed_part, 'rep', axis=2, tiled=True)]
    all_to_all x2, waiting for transfers between devices: 65.8 us -> 37.9 us  [exchange(): lax.all_to_all(sent, 'own', split_axis=0, concat_axis=0, tiled=True)]
    psum x1 -> x2, waiting for transfers between devices: 84.6 us -> 78.6 us  [the longest x1 78.6 us: local(): jax.lax.psum(local_factor, 'own')]
  transfers between devices with their start and end apart: 6 -> 7, of which waited for: 3 -> 3; matrix products, arithmetic and copies ran while one was open for 12% -> 10% of each run, Pallas kernels for 0% -> 0%
where the time goes in v1:
time: 249 us
  waiting for transfers between devices  166 us (67%)
  other arithmetic  25.1 us (10%)
  between operations  15.9 us (6%)
  blocking collectives  12.9 us (5%)
  local copies, waits for them, and re-layouts  11.3 us (5%)
  starting transfers between devices  9.95 us (4%)
  matrix products  7.97 us (3%)
    psum x1, waiting for transfers between devices, local(): jax.lax.psum(local_factor, 'own')  78.6 us
    all_gather x1, waiting for transfers between devices, local(): weight_mean = lax.all_gather(placed_part, 'rep', axis=2, tiled=True)  48 us
    all_to_all x2, waiting for transfers between devices, exchange(): lax.all_to_all(sent, 'own', split_axis=0, concat_axis=0, tiled=True)  37.9 us
    psum x1, blocking collectives, local(): sketch_mean = lax.psum(local_sketch, 'rep') * (1.0 / rep_count)  12.9 us
    select_n x1, other arithmetic, local(): new_momentum = jnp.where(is_filled[:, None, None], moved, 0.0)  11 us
    all_to_all x2, starting transfers between devices, exchange(): lax.all_to_all(sent, 'own', split_axis=0, concat_axis=0, tiled=True)  9.75 us
  transfers between devices with their start and end apart: 7, of which 3 were waited for; matrix products, arithmetic and copies ran while one was open for 10% of the time, Pallas kernels for 0%

profile of v1, /device:TPU:0, one launch (start us, length us, event | category | flops | bytes accessed | tf_op | source)
XLA Modules:
  0.0 248.6 jit_solution(1214205254335328672)
XLA Ops:
  8.0 0.0 copy-start
  8.0 0.0 copy-start.2
  8.0 0.0 copy-start.1
  8.0 0.0 copy-start.5
  8.0 0.0 all-reduce.3.cloned.1.call-start
  8.1 1.0 copy-done
  9.0 2.7 %convolution_bitcast_fusion = f32[64,128]{1,0:T(8,128)S(1)} fusion(f32[64,2048]{1,0:T(8,128)S(1)} %copy-done, f32[128,2048]{1,0:T(8,128)} %param.16, f32[1,128,2048]{2,1,0:T(8,128)} %param.15), kind=kOutput, calls=%fused_computation.6 | convolution fusion | flops 201588736 | bytes 2654208 | tf_op jit(solution)/shard_map/dot_general | solution.py:88
  11.8 12.9 %psum.21 = f32[64,128]{1,0:T(8,128)S(1)} all-reduce(f32[64,128]{1,0:T(8,128)S(1)} %convolution_bitcast_fusion), channel_id=1, replica_groups=mesh['rep'=4,'own'=8] {'rep'}, use_global_device_ids=true, to_apply=%region_7.9 | all-reduce | flops 8192 | bytes 65536 | tf_op jit(solution)/shard_map/psum | solution.py:95
  24.6 0.0 copy-done.5
  24.6 0.2 fusion.7
  24.8 0.0 copy-done.2
  24.8 0.0 copy-done.1
  24.8 1.5 fusion.2
  26.4 0.0 copy-start.6
  26.4 0.0 all-reduce.3.cloned.1.call-update
  26.4 0.0 reduce-scatter.2.cloned.1.call-start
  26.4 0.5 reduce-scatter.2.cloned.1.call-update
  27.0 0.1 copy-done.6
  27.0 0.3 convert_reduce_fusion.1
  27.3 0.3 select_reduce_fusion.1
  27.6 0.1 copy.13
  27.7 0.1 reshape.229
  27.8 3.6 %multiply_subtract_fusion = f32[104,8,512]{2,1,0:T(8,128)} fusion(f32[104,8,2048]{2,1,0:T(8,128)} %param.13, s32[]{:T(128)S(6)} %select_n.88, f32[104,8,2048]{2,1,0:T(8,128)} %param.12), kind=kLoop, calls=%fused_computation.5 | loop fusion | flops 2129920 | bytes 5111812 | tf_op jit(solution)/shard_map/sub | solution.py:69
  31.4 2.2 gather_fusion.2
  33.6 1.4 broadcast_select_fusion.1
  35.0 5.8 %all-to-all-start = ((f32[8,13,8,512]{3,2,1,0:T(8,128)}), f32[8,13,8,512]{3,2,1,0:T(8,128)S(1)}, u32[]{:S(2)}, u32[]{:S(2)}) async-start(f32[8,13,8,512]{3,2,1,0:T(8,128)} %bitcast), calls=%async_computation | async-start | bytes 3407872 | tf_op jit(solution)/shard_map/all_to_all | solution.py:75
  40.9 0.0 all-reduce.5.cloned.1.call-start
  40.9 0.1 compare_and_fusion.3
  41.0 0.3 select_reduce_fusion.2
  41.3 0.1 copy.15
  41.4 0.1 reshape.232
  41.5 0.1 copy.14
  41.6 78.6 %all-reduce.3.cloned.1.call-done = f32[64,2048]{1,0:T(8,128)} async-done(((f32[64,2048]{1,0:T(8,128)}), f32[64,2048]{1,0:T(8,128)}) %all-reduce.3.cloned.1.call-update) | async-done | bytes 524304 | tf_op jit(solution)/shard_map/psum | solution.py:102
  120.2 0.0 all-reduce.5.cloned.1.call-update
  120.3 0.0 all-to-all-done
  120.3 1.4 gather_fusion
  121.6 0.0 reduce-scatter.2.cloned.1.call-done
  121.6 2.1 broadcast_multiply_fusion
  123.8 1.9 gather_fusion.1
  125.7 2.8 %broadcast_select_fusion.2 = f32[8,13,8,512]{3,2,1,0:T(8,128)} fusion(f32[8,13,8,512]{3,2,1,0:T(8,128)} %bitcast.17, pred[8,13]{1,0:T(8,128)(4,1)S(1)} %copy.14), kind=kLoop, calls=%fused_computation.12 | loop fusion | flops 425984 | bytes 3407976 | tf_op jit(solution)/shard_map/jit(_take)/select_n | solution.py:74
  128.5 3.9 %all-to-all-start.1 = ((f32[8,13,8,512]{3,2,1,0:T(8,128)}), f32[8,13,8,512]{3,2,1,0:T(8,128)S(1)}, u32[]{:S(2)}, u32[]{:S(2)}) async-start(f32[8,13,8,512]{3,2,1,0:T(8,128)} %broadcast_select_fusion.2), calls=%async_computation.2 | async-start | bytes 3407872 | tf_op jit(solution)/shard_map/all_to_all | solution.py:75
  132.4 0.0 all-gather.3.cloned.1.call-start
  132.5 0.5 all-gather.3.cloned.1.call-update
  133.0 0.0 all-gather.5.cloned.1.call-start
  133.1 0.1 select_reduce_fusion
  133.2 37.9 %all-to-all-done.1 = f32[8,13,8,512]{3,2,1,0:T(8,128)S(1)} async-done(((f32[8,13,8,512]{3,2,1,0:T(8,128)}), f32[8,13,8,512]{3,2,1,0:T(8,128)S(1)}, u32[]{:S(2)}, u32[]{:S(2)}) %all-to-all-start.1) | async-done | bytes 1703968 | tf_op jit(solution)/shard_map/all_to_all | solution.py:75
  171.1 1.9 gather_fusion.3
  173.0 2.8 %broadcast_select_fusion = f32[104,8,512]{2,1,0:T(8,128)} fusion(f32[104,8,512]{2,1,0:T(8,128)} %gather_fusion.3, pred[104]{0:T(512)(128)(4,1)S(1)} %compare_and_fusion.1), kind=kLoop, calls=%fused_computation.10 | loop fusion | flops 425984 | bytes 3407976 | tf_op jit(solution)/shard_map/jit(_take)/select_n | solution.py:81
  175.8 0.0 copy-start.4
  175.8 0.0 all-gather.5.cloned.1.call-update
  175.9 0.1 fusion.6
  176.0 0.0 all-reduce.5.cloned.1.call-done
  176.0 1.1 copy-done.4
  177.1 3.6 %multiply_subtract_fusion.1 = (f32[128,2048]{1,0:T(8,128)}, f32[128,2048]{1,0:T(8,128)}) fusion(f32[128,2048]{1,0:T(8,128)S(1)} %copy-done.1, f32[128,2048]{1,0:T(8,128)S(1)} %copy-done.4, f32[128,64]{0,1:T(8,128)S(1)} %fusion.7, f32[64,2048]{1,0:T(8,128)} %all-reduce.5.cloned.1.call-done), kind=kOutput, calls=%fused_computation.8 | convolution fusion | flops 203030528 | bytes 4751360 | tf_op jit(solution)/shard_map/dot_general | solution.py:103
  180.6 0.0 all-gather.3.cloned.1.call-done
  180.6 48.0 %all-gather.5.cloned.1.call-done = f32[104,8,2048]{2,1,0:T(8,128)} async-done(((f32[104,8,512]{2,1,0:T(8,128)}), f32[104,8,2048]{2,1,0:T(8,128)}) %all-gather.5.cloned.1.call-update) | async-done | bytes 6815760 | tf_op jit(solution)/shard_map/all_gather | solution.py:83
  228.6 0.0 copy-start.3
  228.6 11.0 %add_select_fusion = f32[104,8,2048]{2,1,0:T(8,128)} fusion(f32[104,8,2048]{2,1,0:T(8,128)} %param.12, f32[104,8,2048]{2,1,0:T(8,128)} %all-gather.5.cloned.1.call-done, f32[104,8,2048]{2,1,0:T(8,128)} %param.13, pred[104]{0:T(512)(128)(4,1)S(1)} %fusion.6), kind=kLoop, calls=%fused_computation.4 | loop fusion | flops 6815744 | bytes 27263080 | tf_op jit(solution)/shard_map/jit(_where)/select_n | solution.py:85
  239.7 0.0 copy-done.3
  239.7 1.3 copy.19
  (17 shorter events, 0.1 us)
Async XLA Ops:
  8.0 1.0 copy-start
  8.0 16.8 %copy-start.2 = (f32[1,128,2048]{2,1,0:T(8,128)S(1)}, f32[1,128,2048]{2,1,0:T(8,128)}, u32[]{:S(2)}) copy-start(f32[1,128,2048]{2,1,0:T(8,128)} %param.15) | copy-start | bytes 3145732
  8.0 16.8 %copy-start.1 = (f32[128,2048]{1,0:T(8,128)S(1)}, f32[128,2048]{1,0:T(8,128)}, u32[]{:S(2)}) copy-start(f32[128,2048]{1,0:T(8,128)} %param.16) | copy-start | bytes 3145732
  8.0 16.6 %copy-start.5 = (f32[64,64]{1,0:T(8,128)S(1)}, f32[64,64]{1,0:T(8,128)}, u32[]{:S(2)}) copy-start(f32[64,64]{1,0:T(8,128)} %param.19) | copy-start | bytes 49156
  8.0 112.2 %all-reduce.3.cloned.1.call-start = ((), (), s32[]{:S(2)}) async-start(), calls=%async_computation.6 | async-start | bytes 1048576 | tf_op jit(solution)/shard_map/psum | solution.py:102
  26.4 0.7 copy-start.6
  26.4 95.3 %reduce-scatter.2.cloned.1.call-start = ((), (), s32[]{:S(2)}) async-start(), calls=%async_computation.3 | async-start | bytes 2621440 | tf_op jit(solution)/shard_map/reduce_scatter | solution.py:64
  35.0 85.2 %all-to-all-start = ((f32[8,13,8,512]{3,2,1,0:T(8,128)}), f32[8,13,8,512]{3,2,1,0:T(8,128)S(1)}, u32[]{:S(2)}, u32[]{:S(2)}) async-start(f32[8,13,8,512]{3,2,1,0:T(8,128)} %bitcast), calls=%async_computation | async-start | bytes 3407872 | tf_op jit(solution)/shard_map/all_to_all | solution.py:75
  40.9 135.1 %all-reduce.5.cloned.1.call-start = ((), (), s32[]{:S(2)}) async-start(), calls=%async_computation.7 | async-start | bytes 1048576 | tf_op jit(solution)/shard_map/psum | solution.py:102
  128.5 42.6 %all-to-all-start.1 = ((f32[8,13,8,512]{3,2,1,0:T(8,128)}), f32[8,13,8,512]{3,2,1,0:T(8,128)S(1)}, u32[]{:S(2)}, u32[]{:S(2)}) async-start(f32[8,13,8,512]{3,2,1,0:T(8,128)} %broadcast_select_fusion.2), calls=%async_computation.2 | async-start | bytes 3407872 | tf_op jit(solution)/shard_map/all_to_all | solution.py:75
  132.4 48.2 %all-gather.3.cloned.1.call-start = ((), (), s32[]{:S(2)}) async-start(), calls=%async_computation.4 | async-start | bytes 2621440 | tf_op jit(solution)/shard_map/all_gather | solution.py:82
  133.0 95.6 %all-gather.5.cloned.1.call-start = ((), (), s32[]{:S(2)}) async-start(), calls=%async_computation.5 | async-start | bytes 8519680 | tf_op jit(solution)/shard_map/all_gather | solution.py:83
  175.8 1.2 copy-start.4
  228.6 11.0 %copy-start.3 = (f32[32,8,2048]{2,1,0:T(8,128)S(1)}, f32[32,8,2048]{2,1,0:T(8,128)}, u32[]{:S(2)}) copy-start(f32[32,8,2048]{2,1,0:T(8,128)} %all-gather.3.cloned.1.call-done) | copy-start | bytes 6291460
Sparse Core Ops, SparseCore 0:
  26.5 93.6 all-reduce.2
Sparse Core Ops, SparseCore 1:
  29.4 31.6 reduce-scatter.1
  120.3 32.4 all-reduce.4
  154.8 22.4 all-gather.2
  179.4 49.2 all-gather.4
